TPU v7x, 1024 devices: a whole 8x8x8 slice. The times are simulated.
1024 devices in a mesh: gx: 8 (over y), gy: 4 (over x_hi), gz: 32 (over z, x_lo, core).
Axes of the slice: x: 8 (x_hi: 4, x_lo: 2; x = x_hi * 2 + x_lo), y: 8, z: 8, core: 2. Of those that a mesh axis runs over, the one named last changes fastest.
Arguments:
- trial: bfloat16 [16, 8, 128, 64, 128], P('gx', 'gy', 'gz'), may hold values from -6 to 6
- onsite: bfloat16 [16, 8, 128, 128, 128], P('gx', 'gy', 'gz'), as said below
- coupling: bfloat16 [3, 16, 8, 128, 128, 128], P(None, 'gx', 'gy', 'gz'), may hold values from -0.1875 to 0.1875
- bonds: int32 [3, 16, 8, 128], P(None, 'gx', 'gy', 'gz'), may hold values 0 or 1
Outputs:
- filtered: float32 [16, 8, 128, 64, 128], P('gx', 'gy', 'gz')
Inputs may be any that keep to these rules, and one draw needn't show every extreme that they name: `onsite`: each on-site block is symmetric in its last two dimensions.
All inputs are finite; a program needn't handle non-finite values. No bound on the sum of `bonds` on one device may be relied on, other than what follows from the above.
Results may differ from a plain program's by a relative error of at most 0.0052.
Values may be sent and summed in bfloat16 or wider, within the bound.
No kernel may reach another device: no remote copies, remote signals or barrier semaphores. Data moves between devices by JAX's collectives and lax.ppermute only.
A program may use at most 32 MiB of HBM per device.

v0:
```python
import jax
import jax.numpy as jnp
from jax import lax
from jax.experimental import pallas as pl
from jax.experimental.pallas import tpu as pltpu
from jax.sharding import PartitionSpec as P


STEPS = 5
CENTER_SHIFT = 0.25
HALF_INVERSE = 0.5

F32 = jnp.float32
BF16 = jnp.bfloat16
AXES = ("gx", "gy", "gz")


def places(lengths):
    nx, ny, nz = lengths
    return [(x, y, z) for x in range(nx) for y in range(ny) for z in range(nz)]


def number(place, lengths):
    return (place[0] * lengths[1] + place[1]) * lengths[2] + place[2]


def stepped(place, axis, by):
    moved = list(place)
    moved[axis] += by
    return tuple(moved)


def face(lengths, axis, layer):
    return [number(p, lengths) for p in places(lengths) if p[axis] == layer]


def plain(vecs, blocks):
    left = vecs[0] if len(vecs) == 1 else jnp.concatenate(vecs, axis=1)
    right = blocks[0] if len(blocks) == 1 else jnp.concatenate(blocks, axis=0)
    return lax.dot_general(left, right, (((1,), (0,)), ((), ())), preferred_element_type=F32)


def crossed(vecs, blocks):
    left = vecs[0] if len(vecs) == 1 else jnp.concatenate(vecs, axis=1)
    right = blocks[0] if len(blocks) == 1 else jnp.concatenate(blocks, axis=1)
    return lax.dot_general(left, right, (((1,), (1,)), ((), ())), preferred_element_type=F32)


def is_even_on(axis):
    return lax.rem(lax.axis_index(AXES[axis]), 2) == 0


def write_messages(lengths, vecs, blocks, sends, axes=(0, 1, 2)):
    for axis in axes:
        low = face(lengths, axis, 0)
        top = face(lengths, axis, lengths[axis] - 1)
        first, second = sends[2 * axis], sends[2 * axis + 1]
        is_even = is_even_on(axis)
        for i in range(len(top)):
            term = plain([vecs[top[i]]], [blocks[axis, top[i]]])
            below = vecs[low[i]].astype(F32)
            first[i] = jnp.where(is_even, term, below).astype(BF16)
            second[i] = jnp.where(is_even, below, term).astype(BF16)


def prepare(lengths, bonds_in, trial_in, coupling_in, vecs, blocks, *refs):
    sends, bonds, vecs_done, bonds_done, blocks_done = refs[:6], refs[6], refs[7], refs[8], refs[9:]
    copies = [pltpu.make_async_copy(bonds_in, bonds, bonds_done)]
    copies.append(pltpu.make_async_copy(trial_in, vecs, vecs_done))
    copies += [pltpu.make_async_copy(coupling_in.at[a], blocks.at[a], blocks_done[a]) for a in range(3)]
    for copy in copies:
        copy.start()
    copies[0].wait()
    copies[1].wait()
    for axis in range(3):
        copies[2 + axis].wait()
        for p in places(lengths):
            c = number(p, lengths)
            blocks[axis, c] = blocks[axis, c] * bonds[axis, p[0], p[1], p[2]].astype(F32).astype(BF16)
        write_messages(lengths, vecs, blocks, sends, (axis,))


def interior(lengths, first_core, vecs, onsite, blocks, *totals):
    total = totals[-1]

    @pl.when(is_even_on(2) == first_core)
    def _():
        interior_sums(lengths, vecs, onsite, blocks, total)


def interior_sums(lengths, vecs, onsite, blocks, total):
    for p in places(lengths):
        c = number(p, lengths)
        vs, ms, ws, ns = [vecs[c]], [onsite[c]], [], []
        for axis in range(3):
            if p[axis] > 0:
                lower = number(stepped(p, axis, -1), lengths)
                vs.append(vecs[lower])
                ms.append(blocks[axis, lower])
            if p[axis] < lengths[axis] - 1:
                upper = number(stepped(p, axis, 1), lengths)
                ws.append(vecs[upper])
                ns.append(blocks[axis, c])
        inside = plain(vs, ms)
        total[c] = inside + crossed(ws, ns) if ws else inside


def finish(lengths, step, total, vecs, previous, blocks, *refs):
    got, result, sends, done = refs[:6], refs[6], refs[7:], None
    if step == STEPS - 1:
        target, result, done, sends = refs[6], refs[7], refs[8], ()
    evens = [is_even_on(axis) for axis in range(3)]
    copies = []
    for p in places(lengths):
        c = number(p, lengths)
        value = total[c]
        ws, ns = [], []
        for axis in range(3):
            is_even = evens[axis]
            first, second = got[2 * axis], got[2 * axis + 1]
            from_above, from_below = (first.at[1], first.at[0]) if axis == 2 else (first, first)
            if p[axis] == lengths[axis] - 1:
                i = face(lengths, axis, p[axis]).index(c)
                ws.append(jnp.where(is_even, from_above[i], second[i]))
                ns.append(blocks[axis, c])
            if p[axis] == 0:
                i = face(lengths, axis, 0).index(c)
                value = value + jnp.where(is_even, second[i], from_below[i]).astype(F32)
        if ws:
            value = value + crossed(ws, ns)
        shifted = value - CENTER_SHIFT * vecs[c].astype(F32)
        if step == 0:
            following = HALF_INVERSE * shifted
        else:
            following = 2.0 * HALF_INVERSE * shifted - previous[c].astype(F32)
        result[c] = following.astype(result.dtype)
        if done is not None and p[2] == lengths[2] - 1:
            run = pl.ds(c + 1 - lengths[2], lengths[2])
            copies.append(pltpu.make_async_copy(result.at[run], target.at[run], done.at[len(copies)]))
            copies[-1].start()
    if sends:
        write_messages(lengths, result, blocks, sends)
    for copy in copies:
        copy.wait()


def call(body, operands, shapes, flops, place=pltpu.VMEM, scratch=(), aliases={}):
    in_specs = [pl.BlockSpec(memory_space=pltpu.VMEM)] * len(operands)
    moved = sum(a.size * a.dtype.itemsize for a in operands) + sum(s.size * s.dtype.itemsize for s in shapes)
    return pl.pallas_call(
        body,
        out_shape=shapes,
        in_specs=in_specs,
        out_specs=[pl.BlockSpec(memory_space=place)] * len(shapes),
        scratch_shapes=scratch,
        input_output_aliases=aliases,
        cost_estimate=pl.CostEstimate(flops=flops, bytes_accessed=moved, transcendentals=0),
        compiler_params=pltpu.CompilerParams(vmem_limit_bytes=24 << 20),
    )(*operands)


def routes(axis):
    n = lax.axis_size(axis)
    pairs = [(i, i + 1) for i in range(0, n - 1, 2)]
    others = [(i, i + 1) for i in range(1, n - 1, 2)]
    both = lambda links: links + [(j, i) for i, j in links]
    return both(pairs), both(others)


def exchanged(sends):
    got = []
    for axis in range(3):
        for which, route in enumerate(routes(AXES[axis])):
            message = sends[2 * axis + which]
            if axis == 2 and which == 0:
                pairs = [[i, i + 1] for i in range(0, lax.axis_size(AXES[axis]), 2)]
                got.append(lax.all_gather(message, AXES[axis], axis_index_groups=pairs))
            else:
                got.append(lax.ppermute(message, AXES[axis], route))
    return got


def shards(trial, onsite, coupling, bonds):
    lengths = trial.shape[:3]
    k, q = trial.shape[3:]
    cells = lengths[0] * lengths[1] * lengths[2]
    vecs = trial.reshape(cells, k, q)
    onsite = onsite.reshape(cells, q, q)
    coupling = coupling.reshape(3, cells, q, q)
    message_shapes = []
    for axis in range(3):
        message_shapes += [jax.ShapeDtypeStruct((cells // lengths[axis], k, q), BF16)] * 2
    one = 2 * k * q * q
    ending = (pltpu.VMEM((cells, k, q), F32), pltpu.SemaphoreType.DMA((lengths[0] * lengths[1],)))
    faces = sum(cells // n for n in lengths)
    shapes = [jax.ShapeDtypeStruct(vecs.shape, BF16), jax.ShapeDtypeStruct(coupling.shape, BF16)] + message_shapes
    vecs, blocks, *sends = pl.pallas_call(
        lambda *r: prepare(lengths, *r),
        out_shape=shapes,
        in_specs=[pl.BlockSpec(memory_space=pltpu.HBM)] * 3,
        out_specs=[pl.BlockSpec(memory_space=pltpu.VMEM)] * len(shapes),
        scratch_shapes=[pltpu.SMEM(bonds.shape, jnp.int32)] + [pltpu.SemaphoreType.DMA] * 5,
        cost_estimate=pl.CostEstimate(flops=faces * one, bytes_accessed=4 << 20, transcendentals=0),
        compiler_params=pltpu.CompilerParams(vmem_limit_bytes=24 << 20),
        name="prepare",
    )(*[pltpu.with_memory_space_constraint(a, pltpu.HBM) for a in (bonds, vecs, coupling)])
    previous = vecs
    for step in range(STEPS):
        last = step == STEPS - 1
        got = exchanged(sends)
        sums, inside = [jax.ShapeDtypeStruct((cells, k, q), F32)], (7 * cells - 2 * faces) * one
        total = call(lambda *r: interior(lengths, False, *r), [vecs, onsite, blocks], sums, inside)
        (total,) = call(
            lambda *r: interior(lengths, True, *r), [vecs, onsite, blocks, *total], sums, inside, aliases={3: 0}
        )
        result = jax.ShapeDtypeStruct((cells, k, q), F32 if last else BF16)
        following, *sends = call(
            lambda *r, step=step: finish(lengths, step, *r),
            [total, vecs, previous, blocks, *got],
            [result] if last else [result] + message_shapes,
            (faces if last else 2 * faces) * one,
            *((pltpu.HBM, ending) if last else ()),
        )
        previous, vecs = vecs, following
    return vecs.reshape(trial.shape)


def solution(mesh):
    placed = (
        P("gx", "gy", "gz", None, None),
        P("gx", "gy", "gz", None, None),
        P(None, "gx", "gy", "gz", None, None),
        P(None, "gx", "gy", "gz"),
    )
    return jax.shard_map(
        shards,
        mesh=mesh,
        in_specs=placed,
        out_specs=P("gx", "gy", "gz", None, None),
        check_vma=False,
    )
```

profile of v0, /device:TPU:407, one launch (start us, length us, event | category | flops | bytes accessed | tf_op | source)
XLA Modules:
  0.0 112.5 jit_solution(7042371880422938618)
XLA Ops:
  0.0 2.2 %prepare.1 = (bf16[16,64,128]{2,1,0:T(8,128)(2,1)S(1)}, bf16[3,16,128,128]{3,2,1,0:T(8,128)(2,1)S(1)}, bf16[8,64,128]{2,1,0:T(8,128)(2,1)S(1)}, bf16[8,64,128]{2...) custom-call(s32[3,2,2,4]{3,2,1,0:T(2,128)} %r_0_.1, ...), custom_call_target="tpu_custom_call" | custom-call | flops 41943040 | bytes 4194304 | tf_op jit(solution)/shard_map/prepare/pallas_call | solution.py:197
  2.2 2.0 %collective-permute-start = (bf16[8,64,128]{2,1,0:T(8,128)(2,1)S(1)}, bf16[8,64,128]{2,1,0:T(8,128)(2,1)S(1)}, u32[]{:S(2)}, u32[]{:S(2)}) collective-permute-start(bf16[8,64,128]{2,1,0:T(8,128)(2,1)S(1)} %get-tuple-element.43), channel_id=1, source_target_pairs={{0,128},{256,384},{512,640},{768,896},{128,0},{384,256},{640,512},... | collective-permute-start | bytes 393224 | tf_op jit(solution)/shard_map/ppermute | solution.py:179
  4.1 4.7 %collective-permute-start.1 = (bf16[8,64,128]{2,1,0:T(8,128)(2,1)S(1)}, bf16[8,64,128]{2,1,0:T(8,128)(2,1)S(1)}, u32[]{:S(2)}, u32[]{:S(2)}) collective-permute-start(bf16[8,64,128]{2,1,0:T(8,128)(2,1)S(1)} %get-tuple-element.44), channel_id=1, source_target_pairs={{128,256},{384,512},{640,768},{256,128},{512,384},{768,640},{129,2... | collective-permute-start | bytes 393224 | tf_op jit(solution)/shard_map/ppermute | solution.py:179
  8.8 2.1 %collective-permute-start.2 = (bf16[8,64,128]{2,1,0:T(8,128)(2,1)S(1)}, bf16[8,64,128]{2,1,0:T(8,128)(2,1)S(1)}, u32[]{:S(2)}, u32[]{:S(2)}) collective-permute-start(bf16[8,64,128]{2,1,0:T(8,128)(2,1)S(1)} %get-tuple-element.45), channel_id=1, source_target_pairs={{0,32},{64,96},{32,0},{96,64},{1,33},{65,97},{33,1},{97,65},{2,34}... | collective-permute-start | bytes 393224 | tf_op jit(solution)/shard_map/ppermute | solution.py:179
  11.0 4.5 %collective-permute-start.3 = (bf16[8,64,128]{2,1,0:T(8,128)(2,1)S(1)}, bf16[8,64,128]{2,1,0:T(8,128)(2,1)S(1)}, u32[]{:S(2)}, u32[]{:S(2)}) collective-permute-start(bf16[8,64,128]{2,1,0:T(8,128)(2,1)S(1)} %get-tuple-element.46), channel_id=1, source_target_pairs={{32,64},{64,32},{33,65},{65,33},{34,66},{66,34},{35,67},{67,35},{3... | collective-permute-start | bytes 393224 | tf_op jit(solution)/shard_map/ppermute | solution.py:179
  15.4 8.7 %collective-permute-start.4 = (bf16[4,64,128]{2,1,0:T(8,128)(2,1)S(1)}, bf16[4,64,128]{2,1,0:T(8,128)(2,1)S(1)}, u32[]{:S(2)}, u32[]{:S(2)}) collective-permute-start(bf16[4,64,128]{2,1,0:T(8,128)(2,1)S(1)} %get-tuple-element.48), channel_id=1, source_target_pairs={{1,2},{3,4},{5,6},{7,8},{9,10},{11,12},{13,14},{15,16},{17,18},{19... | collective-permute-start | bytes 196616 | tf_op jit(solution)/shard_map/ppermute | solution.py:179
  24.1 0.7 shard_map.46.r_3_
  24.9 1.9 %all-gather = bf16[8,64,128]{2,1,0:T(8,128)(2,1)S(1)} all-gather(bf16[4,64,128]{2,1,0:T(8,128)(2,1)S(1)} %get-tuple-element.47), channel_id=2, replica_groups={{0,1},{2,3},{4,5},{6,7},{8,9},{10,11},{12,13},{14,15},{16,17},{18,19},{..., dimensions={0}, use_global_device_ids=true | all-gather | bytes 196608 | tf_op jit(solution)/shard_map/all_gather | solution.py:177
  26.8 1.0 collective-permute-done.4.r_9_
  27.8 0.0 collective-permute-done.r_4_
  27.8 0.0 collective-permute-done.1.r_5_
  27.8 0.0 collective-permute-done.2.r_6_
  27.8 0.0 collective-permute-done.3.r_7_
  27.8 0.7 shard_map.48
  28.5 1.9 %collective-permute-start.5 = (bf16[8,64,128]{2,1,0:T(8,128)(2,1)S(1)}, bf16[8,64,128]{2,1,0:T(8,128)(2,1)S(1)}, u32[]{:S(2)}, u32[]{:S(2)}) collective-permute-start(bf16[8,64,128]{2,1,0:T(8,128)(2,1)S(1)} %get-tuple-element.50), channel_id=1, source_target_pairs={{0,128},{256,384},{512,640},{768,896},{128,0},{384,256},{640,512},... | collective-permute-start | bytes 393224 | tf_op jit(solution)/shard_map/ppermute | solution.py:179
  30.4 5.0 %collective-permute-start.6 = (bf16[8,64,128]{2,1,0:T(8,128)(2,1)S(1)}, bf16[8,64,128]{2,1,0:T(8,128)(2,1)S(1)}, u32[]{:S(2)}, u32[]{:S(2)}) collective-permute-start(bf16[8,64,128]{2,1,0:T(8,128)(2,1)S(1)} %get-tuple-element.51), channel_id=1, source_target_pairs={{128,256},{384,512},{640,768},{256,128},{512,384},{768,640},{129,2... | collective-permute-start | bytes 393224 | tf_op jit(solution)/shard_map/ppermute | solution.py:179
  35.5 1.9 %collective-permute-start.7 = (bf16[8,64,128]{2,1,0:T(8,128)(2,1)S(1)}, bf16[8,64,128]{2,1,0:T(8,128)(2,1)S(1)}, u32[]{:S(2)}, u32[]{:S(2)}) collective-permute-start(bf16[8,64,128]{2,1,0:T(8,128)(2,1)S(1)} %get-tuple-element.52), channel_id=1, source_target_pairs={{0,32},{64,96},{32,0},{96,64},{1,33},{65,97},{33,1},{97,65},{2,34}... | collective-permute-start | bytes 393224 | tf_op jit(solution)/shard_map/ppermute | solution.py:179
  37.4 1.9 %collective-permute-start.8 = (bf16[8,64,128]{2,1,0:T(8,128)(2,1)S(1)}, bf16[8,64,128]{2,1,0:T(8,128)(2,1)S(1)}, u32[]{:S(2)}, u32[]{:S(2)}) collective-permute-start(bf16[8,64,128]{2,1,0:T(8,128)(2,1)S(1)} %get-tuple-element.53), channel_id=1, source_target_pairs={{32,64},{64,32},{33,65},{65,33},{34,66},{66,34},{35,67},{67,35},{3... | collective-permute-start | bytes 393224 | tf_op jit(solution)/shard_map/ppermute | solution.py:179
  39.3 5.6 %collective-permute-start.9 = (bf16[4,64,128]{2,1,0:T(8,128)(2,1)S(1)}, bf16[4,64,128]{2,1,0:T(8,128)(2,1)S(1)}, u32[]{:S(2)}, u32[]{:S(2)}) collective-permute-start(bf16[4,64,128]{2,1,0:T(8,128)(2,1)S(1)} %get-tuple-element.55), channel_id=1, source_target_pairs={{1,2},{3,4},{5,6},{7,8},{9,10},{11,12},{13,14},{15,16},{17,18},{19... | collective-permute-start | bytes 196616 | tf_op jit(solution)/shard_map/ppermute | solution.py:179
  44.9 0.7 shard_map.49.r_3_
  45.7 1.9 %all-gather.1 = bf16[8,64,128]{2,1,0:T(8,128)(2,1)S(1)} all-gather(bf16[4,64,128]{2,1,0:T(8,128)(2,1)S(1)} %get-tuple-element.54), channel_id=3, replica_groups={{0,1},{2,3},{4,5},{6,7},{8,9},{10,11},{12,13},{14,15},{16,17},{18,19},{..., dimensions={0}, use_global_device_ids=true | all-gather | bytes 196608 | tf_op jit(solution)/shard_map/all_gather | solution.py:177
  47.6 2.0 %collective-permute-done.9.r_9_ = bf16[4,64,128]{2,1,0:T(8,128)(2,1)S(1)} collective-permute-done((bf16[4,64,128]{2,1,0:T(8,128)(2,1)S(1)}, bf16[4,64,128]{2,1,0:T(8,128)(2,1)S(1)}, u32[]{:S(2)}, u32[]{:S(2)}) %collective-permute-start.9) | collective-permute-done | bytes 65568 | tf_op jit(solution)/shard_map/ppermute | solution.py:179
  49.6 0.0 collective-permute-done.5.r_4_
  49.6 0.0 collective-permute-done.6.r_5_
  49.6 0.0 collective-permute-done.7.r_6_
  49.6 0.0 collective-permute-done.8.r_7_
  49.6 0.7 shard_map.51
  50.3 1.9 %collective-permute-start.10 = (bf16[8,64,128]{2,1,0:T(8,128)(2,1)S(1)}, bf16[8,64,128]{2,1,0:T(8,128)(2,1)S(1)}, u32[]{:S(2)}, u32[]{:S(2)}) collective-permute-start(bf16[8,64,128]{2,1,0:T(8,128)(2,1)S(1)} %get-tuple-element.57), channel_id=1, source_target_pairs={{0,128},{256,384},{512,640},{768,896},{128,0},{384,256},{640,512},... | collective-permute-start | bytes 393224 | tf_op jit(solution)/shard_map/ppermute | solution.py:179
  52.2 2.9 %collective-permute-start.11 = (bf16[8,64,128]{2,1,0:T(8,128)(2,1)S(1)}, bf16[8,64,128]{2,1,0:T(8,128)(2,1)S(1)}, u32[]{:S(2)}, u32[]{:S(2)}) collective-permute-start(bf16[8,64,128]{2,1,0:T(8,128)(2,1)S(1)} %get-tuple-element.58), channel_id=1, source_target_pairs={{128,256},{384,512},{640,768},{256,128},{512,384},{768,640},{129,2... | collective-permute-start | bytes 393224 | tf_op jit(solution)/shard_map/ppermute | solution.py:179
  55.1 1.9 %collective-permute-start.12 = (bf16[8,64,128]{2,1,0:T(8,128)(2,1)S(1)}, bf16[8,64,128]{2,1,0:T(8,128)(2,1)S(1)}, u32[]{:S(2)}, u32[]{:S(2)}) collective-permute-start(bf16[8,64,128]{2,1,0:T(8,128)(2,1)S(1)} %get-tuple-element.59), channel_id=1, source_target_pairs={{0,32},{64,96},{32,0},{96,64},{1,33},{65,97},{33,1},{97,65},{2,34}... | collective-permute-start | bytes 393224 | tf_op jit(solution)/shard_map/ppermute | solution.py:179
  57.1 3.8 %collective-permute-start.13 = (bf16[8,64,128]{2,1,0:T(8,128)(2,1)S(1)}, bf16[8,64,128]{2,1,0:T(8,128)(2,1)S(1)}, u32[]{:S(2)}, u32[]{:S(2)}) collective-permute-start(bf16[8,64,128]{2,1,0:T(8,128)(2,1)S(1)} %get-tuple-element.60), channel_id=1, source_target_pairs={{32,64},{64,32},{33,65},{65,33},{34,66},{66,34},{35,67},{67,35},{3... | collective-permute-start | bytes 393224 | tf_op jit(solution)/shard_map/ppermute | solution.py:179
  60.8 4.9 %collective-permute-start.14 = (bf16[4,64,128]{2,1,0:T(8,128)(2,1)S(1)}, bf16[4,64,128]{2,1,0:T(8,128)(2,1)S(1)}, u32[]{:S(2)}, u32[]{:S(2)}) collective-permute-start(bf16[4,64,128]{2,1,0:T(8,128)(2,1)S(1)} %get-tuple-element.62), channel_id=1, source_target_pairs={{1,2},{3,4},{5,6},{7,8},{9,10},{11,12},{13,14},{15,16},{17,18},{19... | collective-permute-start | bytes 196616 | tf_op jit(solution)/shard_map/ppermute | solution.py:179
  65.7 0.7 shard_map.52.r_3_
  66.5 1.9 %all-gather.2 = bf16[8,64,128]{2,1,0:T(8,128)(2,1)S(1)} all-gather(bf16[4,64,128]{2,1,0:T(8,128)(2,1)S(1)} %get-tuple-element.61), channel_id=4, replica_groups={{0,1},{2,3},{4,5},{6,7},{8,9},{10,11},{12,13},{14,15},{16,17},{18,19},{..., dimensions={0}, use_global_device_ids=true | all-gather | bytes 196608 | tf_op jit(solution)/shard_map/all_gather | solution.py:177
  68.4 2.1 %collective-permute-done.14.r_9_ = bf16[4,64,128]{2,1,0:T(8,128)(2,1)S(1)} collective-permute-done((bf16[4,64,128]{2,1,0:T(8,128)(2,1)S(1)}, bf16[4,64,128]{2,1,0:T(8,128)(2,1)S(1)}, u32[]{:S(2)}, u32[]{:S(2)}) %collective-permute-start.14) | collective-permute-done | bytes 65568 | tf_op jit(solution)/shard_map/ppermute | solution.py:179
  70.5 0.0 collective-permute-done.10.r_4_
  70.5 0.0 collective-permute-done.11.r_5_
  70.5 0.0 collective-permute-done.12.r_6_
  70.5 0.0 collective-permute-done.13.r_7_
  70.5 0.7 shard_map.54
  71.2 1.9 %collective-permute-start.15 = (bf16[8,64,128]{2,1,0:T(8,128)(2,1)S(1)}, bf16[8,64,128]{2,1,0:T(8,128)(2,1)S(1)}, u32[]{:S(2)}, u32[]{:S(2)}) collective-permute-start(bf16[8,64,128]{2,1,0:T(8,128)(2,1)S(1)} %get-tuple-element.64), channel_id=1, source_target_pairs={{0,128},{256,384},{512,640},{768,896},{128,0},{384,256},{640,512},... | collective-permute-start | bytes 393224 | tf_op jit(solution)/shard_map/ppermute | solution.py:179
  73.1 3.4 %collective-permute-start.16 = (bf16[8,64,128]{2,1,0:T(8,128)(2,1)S(1)}, bf16[8,64,128]{2,1,0:T(8,128)(2,1)S(1)}, u32[]{:S(2)}, u32[]{:S(2)}) collective-permute-start(bf16[8,64,128]{2,1,0:T(8,128)(2,1)S(1)} %get-tuple-element.65), channel_id=1, source_target_pairs={{128,256},{384,512},{640,768},{256,128},{512,384},{768,640},{129,2... | collective-permute-start | bytes 393224 | tf_op jit(solution)/shard_map/ppermute | solution.py:179
  76.5 1.9 %collective-permute-start.17 = (bf16[8,64,128]{2,1,0:T(8,128)(2,1)S(1)}, bf16[8,64,128]{2,1,0:T(8,128)(2,1)S(1)}, u32[]{:S(2)}, u32[]{:S(2)}) collective-permute-start(bf16[8,64,128]{2,1,0:T(8,128)(2,1)S(1)} %get-tuple-element.66), channel_id=1, source_target_pairs={{0,32},{64,96},{32,0},{96,64},{1,33},{65,97},{33,1},{97,65},{2,34}... | collective-permute-start | bytes 393224 | tf_op jit(solution)/shard_map/ppermute | solution.py:179
  78.4 2.6 %collective-permute-start.18 = (bf16[8,64,128]{2,1,0:T(8,128)(2,1)S(1)}, bf16[8,64,128]{2,1,0:T(8,128)(2,1)S(1)}, u32[]{:S(2)}, u32[]{:S(2)}) collective-permute-start(bf16[8,64,128]{2,1,0:T(8,128)(2,1)S(1)} %get-tuple-element.67), channel_id=1, source_target_pairs={{32,64},{64,32},{33,65},{65,33},{34,66},{66,34},{35,67},{67,35},{3... | collective-permute-start | bytes 393224 | tf_op jit(solution)/shard_map/ppermute | solution.py:179
  81.0 4.9 %collective-permute-start.19 = (bf16[4,64,128]{2,1,0:T(8,128)(2,1)S(1)}, bf16[4,64,128]{2,1,0:T(8,128)(2,1)S(1)}, u32[]{:S(2)}, u32[]{:S(2)}) collective-permute-start(bf16[4,64,128]{2,1,0:T(8,128)(2,1)S(1)} %get-tuple-element.69), channel_id=1, source_target_pairs={{1,2},{3,4},{5,6},{7,8},{9,10},{11,12},{13,14},{15,16},{17,18},{19... | collective-permute-start | bytes 196616 | tf_op jit(solution)/shard_map/ppermute | solution.py:179
  85.9 0.7 shard_map.55.r_3_
  86.7 1.9 %all-gather.3 = bf16[8,64,128]{2,1,0:T(8,128)(2,1)S(1)} all-gather(bf16[4,64,128]{2,1,0:T(8,128)(2,1)S(1)} %get-tuple-element.68), channel_id=5, replica_groups={{0,1},{2,3},{4,5},{6,7},{8,9},{10,11},{12,13},{14,15},{16,17},{18,19},{..., dimensions={0}, use_global_device_ids=true | all-gather | bytes 196608 | tf_op jit(solution)/shard_map/all_gather | solution.py:177
  88.6 1.8 %collective-permute-done.19.r_9_ = bf16[4,64,128]{2,1,0:T(8,128)(2,1)S(1)} collective-permute-done((bf16[4,64,128]{2,1,0:T(8,128)(2,1)S(1)}, bf16[4,64,128]{2,1,0:T(8,128)(2,1)S(1)}, u32[]{:S(2)}, u32[]{:S(2)}) %collective-permute-start.19) | collective-permute-done | bytes 65568 | tf_op jit(solution)/shard_map/ppermute | solution.py:179
  90.3 0.0 collective-permute-done.15.r_4_
  90.3 0.0 collective-permute-done.16.r_5_
  90.4 0.0 collective-permute-done.18.r_7_
  90.4 0.7 shard_map.57
  91.1 1.9 %collective-permute-start.20 = (bf16[8,64,128]{2,1,0:T(8,128)(2,1)S(1)}, bf16[8,64,128]{2,1,0:T(8,128)(2,1)S(1)}, u32[]{:S(2)}, u32[]{:S(2)}) collective-permute-start(bf16[8,64,128]{2,1,0:T(8,128)(2,1)S(1)} %get-tuple-element.71), channel_id=1, source_target_pairs={{0,128},{256,384},{512,640},{768,896},{128,0},{384,256},{640,512},... | collective-permute-start | bytes 393224 | tf_op jit(solution)/shard_map/ppermute | solution.py:179
  93.0 3.7 %collective-permute-start.21 = (bf16[8,64,128]{2,1,0:T(8,128)(2,1)S(1)}, bf16[8,64,128]{2,1,0:T(8,128)(2,1)S(1)}, u32[]{:S(2)}, u32[]{:S(2)}) collective-permute-start(bf16[8,64,128]{2,1,0:T(8,128)(2,1)S(1)} %get-tuple-element.72), channel_id=1, source_target_pairs={{128,256},{384,512},{640,768},{256,128},{512,384},{768,640},{129,2... | collective-permute-start | bytes 393224 | tf_op jit(solution)/shard_map/ppermute | solution.py:179
  96.7 1.9 %collective-permute-start.22 = (bf16[8,64,128]{2,1,0:T(8,128)(2,1)S(1)}, bf16[8,64,128]{2,1,0:T(8,128)(2,1)S(1)}, u32[]{:S(2)}, u32[]{:S(2)}) collective-permute-start(bf16[8,64,128]{2,1,0:T(8,128)(2,1)S(1)} %get-tuple-element.73), channel_id=1, source_target_pairs={{0,32},{64,96},{32,0},{96,64},{1,33},{65,97},{33,1},{97,65},{2,34}... | collective-permute-start | bytes 393224 | tf_op jit(solution)/shard_map/ppermute | solution.py:179
  98.6 2.8 %collective-permute-start.23 = (bf16[8,64,128]{2,1,0:T(8,128)(2,1)S(1)}, bf16[8,64,128]{2,1,0:T(8,128)(2,1)S(1)}, u32[]{:S(2)}, u32[]{:S(2)}) collective-permute-start(bf16[8,64,128]{2,1,0:T(8,128)(2,1)S(1)} %get-tuple-element.74), channel_id=1, source_target_pairs={{32,64},{64,32},{33,65},{65,33},{34,66},{66,34},{35,67},{67,35},{3... | collective-permute-start | bytes 393224 | tf_op jit(solution)/shard_map/ppermute | solution.py:179
  101.5 5.3 %collective-permute-start.24 = (bf16[4,64,128]{2,1,0:T(8,128)(2,1)S(1)}, bf16[4,64,128]{2,1,0:T(8,128)(2,1)S(1)}, u32[]{:S(2)}, u32[]{:S(2)}) collective-permute-start(bf16[4,64,128]{2,1,0:T(8,128)(2,1)S(1)} %get-tuple-element.76), channel_id=1, source_target_pairs={{1,2},{3,4},{5,6},{7,8},{9,10},{11,12},{13,14},{15,16},{17,18},{19... | collective-permute-start | bytes 196616 | tf_op jit(solution)/shard_map/ppermute | solution.py:179
  106.7 0.7 shard_map.58.r_3_
  107.5 1.9 %all-gather.4 = bf16[8,64,128]{2,1,0:T(8,128)(2,1)S(1)} all-gather(bf16[4,64,128]{2,1,0:T(8,128)(2,1)S(1)} %get-tuple-element.75), channel_id=6, replica_groups={{0,1},{2,3},{4,5},{6,7},{8,9},{10,11},{12,13},{14,15},{16,17},{18,19},{..., dimensions={0}, use_global_device_ids=true | all-gather | bytes 196608 | tf_op jit(solution)/shard_map/all_gather | solution.py:177
  109.4 1.9 %collective-permute-done.24.r_9_ = bf16[4,64,128]{2,1,0:T(8,128)(2,1)S(1)} collective-permute-done((bf16[4,64,128]{2,1,0:T(8,128)(2,1)S(1)}, bf16[4,64,128]{2,1,0:T(8,128)(2,1)S(1)}, u32[]{:S(2)}, u32[]{:S(2)}) %collective-permute-start.24) | collective-permute-done | bytes 65568 | tf_op jit(solution)/shard_map/ppermute | solution.py:179
  111.3 0.0 collective-permute-done.20.r_4_
  111.3 0.0 collective-permute-done.21.r_5_
  111.3 0.0 collective-permute-done.22.r_6_
  111.3 1.1 %shard_map.60 = f32[16,64,128]{2,1,0:T(8,128)} custom-call(f32[16,64,128]{2,1,0:T(8,128)S(1)} %shard_map.59.r_0_, bf16[16,64,128]{2,1,0:T(8,128)(2,1)S(1)} %get-tuple-element.70.r_0_.r_1_, bf16[16,64,128]{2,1,0:T(8,128)(2,1)S(1)} %get-tuple-element.63.r_0_.r_1_.r_2_, bf16[3,16,128,128]{3,2,1,0:T(8,128)(2,1)S(1)} %get-tuple-element.42.r_2_.r_3_, ...), custom_call_target="tpu_custom_call" | custom-call | flops 41943040 | bytes 3866624 | tf_op jit(solution)/shard_map/pallas_call | solution.py:150
  (9 shorter events, 0.1 us)
Async XLA Ops:
  0.0 24.1 %copy-start = (bf16[2,2,4,128,128]{4,3,2,1,0:T(8,128)(2,1)S(1)}, bf16[2,2,4,128,128]{4,3,2,1,0:T(8,128)(2,1)}, u32[]{:S(2)}) copy-start(bf16[2,2,4,128,128]{4,3,2,1,0:T(8,128)(2,1)} %param.5) | copy-start | bytes 1572868
  2.2 25.6 %collective-permute-start = (bf16[8,64,128]{2,1,0:T(8,128)(2,1)S(1)}, bf16[8,64,128]{2,1,0:T(8,128)(2,1)S(1)}, u32[]{:S(2)}, u32[]{:S(2)}) collective-permute-start(bf16[8,64,128]{2,1,0:T(8,128)(2,1)S(1)} %get-tuple-element.43), channel_id=1, source_target_pairs={{0,128},{256,384},{512,640},{768,896},{128,0},{384,256},{640,512},... | collective-permute-start | bytes 393224 | tf_op jit(solution)/shard_map/ppermute | solution.py:179
  4.1 23.7 %collective-permute-start.1 = (bf16[8,64,128]{2,1,0:T(8,128)(2,1)S(1)}, bf16[8,64,128]{2,1,0:T(8,128)(2,1)S(1)}, u32[]{:S(2)}, u32[]{:S(2)}) collective-permute-start(bf16[8,64,128]{2,1,0:T(8,128)(2,1)S(1)} %get-tuple-element.44), channel_id=1, source_target_pairs={{128,256},{384,512},{640,768},{256,128},{512,384},{768,640},{129,2... | collective-permute-start | bytes 393224 | tf_op jit(solution)/shard_map/ppermute | solution.py:179
  8.8 19.0 %collective-permute-start.2 = (bf16[8,64,128]{2,1,0:T(8,128)(2,1)S(1)}, bf16[8,64,128]{2,1,0:T(8,128)(2,1)S(1)}, u32[]{:S(2)}, u32[]{:S(2)}) collective-permute-start(bf16[8,64,128]{2,1,0:T(8,128)(2,1)S(1)} %get-tuple-element.45), channel_id=1, source_target_pairs={{0,32},{64,96},{32,0},{96,64},{1,33},{65,97},{33,1},{97,65},{2,34}... | collective-permute-start | bytes 393224 | tf_op jit(solution)/shard_map/ppermute | solution.py:179
  11.0 16.9 %collective-permute-start.3 = (bf16[8,64,128]{2,1,0:T(8,128)(2,1)S(1)}, bf16[8,64,128]{2,1,0:T(8,128)(2,1)S(1)}, u32[]{:S(2)}, u32[]{:S(2)}) collective-permute-start(bf16[8,64,128]{2,1,0:T(8,128)(2,1)S(1)} %get-tuple-element.46), channel_id=1, source_target_pairs={{32,64},{64,32},{33,65},{65,33},{34,66},{66,34},{35,67},{67,35},{3... | collective-permute-start | bytes 393224 | tf_op jit(solution)/shard_map/ppermute | solution.py:179
  15.4 12.4 %collective-permute-start.4 = (bf16[4,64,128]{2,1,0:T(8,128)(2,1)S(1)}, bf16[4,64,128]{2,1,0:T(8,128)(2,1)S(1)}, u32[]{:S(2)}, u32[]{:S(2)}) collective-permute-start(bf16[4,64,128]{2,1,0:T(8,128)(2,1)S(1)} %get-tuple-element.48), channel_id=1, source_target_pairs={{1,2},{3,4},{5,6},{7,8},{9,10},{11,12},{13,14},{15,16},{17,18},{19... | collective-permute-start | bytes 196616 | tf_op jit(solution)/shard_map/ppermute | solution.py:179
  28.5 21.1 %collective-permute-start.5 = (bf16[8,64,128]{2,1,0:T(8,128)(2,1)S(1)}, bf16[8,64,128]{2,1,0:T(8,128)(2,1)S(1)}, u32[]{:S(2)}, u32[]{:S(2)}) collective-permute-start(bf16[8,64,128]{2,1,0:T(8,128)(2,1)S(1)} %get-tuple-element.50), channel_id=1, source_target_pairs={{0,128},{256,384},{512,640},{768,896},{128,0},{384,256},{640,512},... | collective-permute-start | bytes 393224 | tf_op jit(solution)/shard_map/ppermute | solution.py:179
  30.4 19.1 %collective-permute-start.6 = (bf16[8,64,128]{2,1,0:T(8,128)(2,1)S(1)}, bf16[8,64,128]{2,1,0:T(8,128)(2,1)S(1)}, u32[]{:S(2)}, u32[]{:S(2)}) collective-permute-start(bf16[8,64,128]{2,1,0:T(8,128)(2,1)S(1)} %get-tuple-element.51), channel_id=1, source_target_pairs={{128,256},{384,512},{640,768},{256,128},{512,384},{768,640},{129,2... | collective-permute-start | bytes 393224 | tf_op jit(solution)/shard_map/ppermute | solution.py:179
  35.5 14.1 %collective-permute-start.7 = (bf16[8,64,128]{2,1,0:T(8,128)(2,1)S(1)}, bf16[8,64,128]{2,1,0:T(8,128)(2,1)S(1)}, u32[]{:S(2)}, u32[]{:S(2)}) collective-permute-start(bf16[8,64,128]{2,1,0:T(8,128)(2,1)S(1)} %get-tuple-element.52), channel_id=1, source_target_pairs={{0,32},{64,96},{32,0},{96,64},{1,33},{65,97},{33,1},{97,65},{2,34}... | collective-permute-start | bytes 393224 | tf_op jit(solution)/shard_map/ppermute | solution.py:179
  37.4 12.2 %collective-permute-start.8 = (bf16[8,64,128]{2,1,0:T(8,128)(2,1)S(1)}, bf16[8,64,128]{2,1,0:T(8,128)(2,1)S(1)}, u32[]{:S(2)}, u32[]{:S(2)}) collective-permute-start(bf16[8,64,128]{2,1,0:T(8,128)(2,1)S(1)} %get-tuple-element.53), channel_id=1, source_target_pairs={{32,64},{64,32},{33,65},{65,33},{34,66},{66,34},{35,67},{67,35},{3... | collective-permute-start | bytes 393224 | tf_op jit(solution)/shard_map/ppermute | solution.py:179
  39.3 10.2 %collective-permute-start.9 = (bf16[4,64,128]{2,1,0:T(8,128)(2,1)S(1)}, bf16[4,64,128]{2,1,0:T(8,128)(2,1)S(1)}, u32[]{:S(2)}, u32[]{:S(2)}) collective-permute-start(bf16[4,64,128]{2,1,0:T(8,128)(2,1)S(1)} %get-tuple-element.55), channel_id=1, source_target_pairs={{1,2},{3,4},{5,6},{7,8},{9,10},{11,12},{13,14},{15,16},{17,18},{19... | collective-permute-start | bytes 196616 | tf_op jit(solution)/shard_map/ppermute | solution.py:179
  50.3 20.2 %collective-permute-start.10 = (bf16[8,64,128]{2,1,0:T(8,128)(2,1)S(1)}, bf16[8,64,128]{2,1,0:T(8,128)(2,1)S(1)}, u32[]{:S(2)}, u32[]{:S(2)}) collective-permute-start(bf16[8,64,128]{2,1,0:T(8,128)(2,1)S(1)} %get-tuple-element.57), channel_id=1, source_target_pairs={{0,128},{256,384},{512,640},{768,896},{128,0},{384,256},{640,512},... | collective-permute-start | bytes 393224 | tf_op jit(solution)/shard_map/ppermute | solution.py:179
  52.2 18.2 %collective-permute-start.11 = (bf16[8,64,128]{2,1,0:T(8,128)(2,1)S(1)}, bf16[8,64,128]{2,1,0:T(8,128)(2,1)S(1)}, u32[]{:S(2)}, u32[]{:S(2)}) collective-permute-start(bf16[8,64,128]{2,1,0:T(8,128)(2,1)S(1)} %get-tuple-element.58), channel_id=1, source_target_pairs={{128,256},{384,512},{640,768},{256,128},{512,384},{768,640},{129,2... | collective-permute-start | bytes 393224 | tf_op jit(solution)/shard_map/ppermute | solution.py:179
  55.1 15.3 %collective-permute-start.12 = (bf16[8,64,128]{2,1,0:T(8,128)(2,1)S(1)}, bf16[8,64,128]{2,1,0:T(8,128)(2,1)S(1)}, u32[]{:S(2)}, u32[]{:S(2)}) collective-permute-start(bf16[8,64,128]{2,1,0:T(8,128)(2,1)S(1)} %get-tuple-element.59), channel_id=1, source_target_pairs={{0,32},{64,96},{32,0},{96,64},{1,33},{65,97},{33,1},{97,65},{2,34}... | collective-permute-start | bytes 393224 | tf_op jit(solution)/shard_map/ppermute | solution.py:179
  57.1 13.4 %collective-permute-start.13 = (bf16[8,64,128]{2,1,0:T(8,128)(2,1)S(1)}, bf16[8,64,128]{2,1,0:T(8,128)(2,1)S(1)}, u32[]{:S(2)}, u32[]{:S(2)}) collective-permute-start(bf16[8,64,128]{2,1,0:T(8,128)(2,1)S(1)} %get-tuple-element.60), channel_id=1, source_target_pairs={{32,64},{64,32},{33,65},{65,33},{34,66},{66,34},{35,67},{67,35},{3... | collective-permute-start | bytes 393224 | tf_op jit(solution)/shard_map/ppermute | solution.py:179
  60.8 9.6 %collective-permute-start.14 = (bf16[4,64,128]{2,1,0:T(8,128)(2,1)S(1)}, bf16[4,64,128]{2,1,0:T(8,128)(2,1)S(1)}, u32[]{:S(2)}, u32[]{:S(2)}) collective-permute-start(bf16[4,64,128]{2,1,0:T(8,128)(2,1)S(1)} %get-tuple-element.62), channel_id=1, source_target_pairs={{1,2},{3,4},{5,6},{7,8},{9,10},{11,12},{13,14},{15,16},{17,18},{19... | collective-permute-start | bytes 196616 | tf_op jit(solution)/shard_map/ppermute | solution.py:179
  71.2 19.2 %collective-permute-start.15 = (bf16[8,64,128]{2,1,0:T(8,128)(2,1)S(1)}, bf16[8,64,128]{2,1,0:T(8,128)(2,1)S(1)}, u32[]{:S(2)}, u32[]{:S(2)}) collective-permute-start(bf16[8,64,128]{2,1,0:T(8,128)(2,1)S(1)} %get-tuple-element.64), channel_id=1, source_target_pairs={{0,128},{256,384},{512,640},{768,896},{128,0},{384,256},{640,512},... | collective-permute-start | bytes 393224 | tf_op jit(solution)/shard_map/ppermute | solution.py:179
  73.1 17.3 %collective-permute-start.16 = (bf16[8,64,128]{2,1,0:T(8,128)(2,1)S(1)}, bf16[8,64,128]{2,1,0:T(8,128)(2,1)S(1)}, u32[]{:S(2)}, u32[]{:S(2)}) collective-permute-start(bf16[8,64,128]{2,1,0:T(8,128)(2,1)S(1)} %get-tuple-element.65), channel_id=1, source_target_pairs={{128,256},{384,512},{640,768},{256,128},{512,384},{768,640},{129,2... | collective-permute-start | bytes 393224 | tf_op jit(solution)/shard_map/ppermute | solution.py:179
  76.5 13.9 %collective-permute-start.17 = (bf16[8,64,128]{2,1,0:T(8,128)(2,1)S(1)}, bf16[8,64,128]{2,1,0:T(8,128)(2,1)S(1)}, u32[]{:S(2)}, u32[]{:S(2)}) collective-permute-start(bf16[8,64,128]{2,1,0:T(8,128)(2,1)S(1)} %get-tuple-element.66), channel_id=1, source_target_pairs={{0,32},{64,96},{32,0},{96,64},{1,33},{65,97},{33,1},{97,65},{2,34}... | collective-permute-start | bytes 393224 | tf_op jit(solution)/shard_map/ppermute | solution.py:179
  78.4 11.9 %collective-permute-start.18 = (bf16[8,64,128]{2,1,0:T(8,128)(2,1)S(1)}, bf16[8,64,128]{2,1,0:T(8,128)(2,1)S(1)}, u32[]{:S(2)}, u32[]{:S(2)}) collective-permute-start(bf16[8,64,128]{2,1,0:T(8,128)(2,1)S(1)} %get-tuple-element.67), channel_id=1, source_target_pairs={{32,64},{64,32},{33,65},{65,33},{34,66},{66,34},{35,67},{67,35},{3... | collective-permute-start | bytes 393224 | tf_op jit(solution)/shard_map/ppermute | solution.py:179
  81.0 9.4 %collective-permute-start.19 = (bf16[4,64,128]{2,1,0:T(8,128)(2,1)S(1)}, bf16[4,64,128]{2,1,0:T(8,128)(2,1)S(1)}, u32[]{:S(2)}, u32[]{:S(2)}) collective-permute-start(bf16[4,64,128]{2,1,0:T(8,128)(2,1)S(1)} %get-tuple-element.69), channel_id=1, source_target_pairs={{1,2},{3,4},{5,6},{7,8},{9,10},{11,12},{13,14},{15,16},{17,18},{19... | collective-permute-start | bytes 196616 | tf_op jit(solution)/shard_map/ppermute | solution.py:179
  91.1 20.2 %collective-permute-start.20 = (bf16[8,64,128]{2,1,0:T(8,128)(2,1)S(1)}, bf16[8,64,128]{2,1,0:T(8,128)(2,1)S(1)}, u32[]{:S(2)}, u32[]{:S(2)}) collective-permute-start(bf16[8,64,128]{2,1,0:T(8,128)(2,1)S(1)} %get-tuple-element.71), channel_id=1, source_target_pairs={{0,128},{256,384},{512,640},{768,896},{128,0},{384,256},{640,512},... | collective-permute-start | bytes 393224 | tf_op jit(solution)/shard_map/ppermute | solution.py:179
  93.0 18.3 %collective-permute-start.21 = (bf16[8,64,128]{2,1,0:T(8,128)(2,1)S(1)}, bf16[8,64,128]{2,1,0:T(8,128)(2,1)S(1)}, u32[]{:S(2)}, u32[]{:S(2)}) collective-permute-start(bf16[8,64,128]{2,1,0:T(8,128)(2,1)S(1)} %get-tuple-element.72), channel_id=1, source_target_pairs={{128,256},{384,512},{640,768},{256,128},{512,384},{768,640},{129,2... | collective-permute-start | bytes 393224 | tf_op jit(solution)/shard_map/ppermute | solution.py:179
  96.7 14.6 %collective-permute-start.22 = (bf16[8,64,128]{2,1,0:T(8,128)(2,1)S(1)}, bf16[8,64,128]{2,1,0:T(8,128)(2,1)S(1)}, u32[]{:S(2)}, u32[]{:S(2)}) collective-permute-start(bf16[8,64,128]{2,1,0:T(8,128)(2,1)S(1)} %get-tuple-element.73), channel_id=1, source_target_pairs={{0,32},{64,96},{32,0},{96,64},{1,33},{65,97},{33,1},{97,65},{2,34}... | collective-permute-start | bytes 393224 | tf_op jit(solution)/shard_map/ppermute | solution.py:179
  98.6 12.7 %collective-permute-start.23 = (bf16[8,64,128]{2,1,0:T(8,128)(2,1)S(1)}, bf16[8,64,128]{2,1,0:T(8,128)(2,1)S(1)}, u32[]{:S(2)}, u32[]{:S(2)}) collective-permute-start(bf16[8,64,128]{2,1,0:T(8,128)(2,1)S(1)} %get-tuple-element.74), channel_id=1, source_target_pairs={{32,64},{64,32},{33,65},{65,33},{34,66},{66,34},{35,67},{67,35},{3... | collective-permute-start | bytes 393224 | tf_op jit(solution)/shard_map/ppermute | solution.py:179
  101.5 9.8 %collective-permute-start.24 = (bf16[4,64,128]{2,1,0:T(8,128)(2,1)S(1)}, bf16[4,64,128]{2,1,0:T(8,128)(2,1)S(1)}, u32[]{:S(2)}, u32[]{:S(2)}) collective-permute-start(bf16[4,64,128]{2,1,0:T(8,128)(2,1)S(1)} %get-tuple-element.76), channel_id=1, source_target_pairs={{1,2},{3,4},{5,6},{7,8},{9,10},{11,12},{13,14},{15,16},{17,18},{19... | collective-permute-start | bytes 196616 | tf_op jit(solution)/shard_map/ppermute | solution.py:179
where the time goes:
time: 113 us; the launch traced here: 112 us
  starting transfers between devices  84 us (74%)
  Pallas kernels  9.77 us (9%)
  blocking collectives  9.5 us (8%)
  waiting for transfers between devices  8.77 us (8%)
    ppermute x25, starting transfers between devices, exchanged(): got.append(lax.ppermute(message, AXES[axis], route))  84 us
    all_gather x5, blocking collectives, exchanged(): got.append(lax.all_gather(message, AXES[axis], axis_index_groups=pairs))  9.5 us
    ppermute x25, waiting for transfers between devices, exchanged(): got.append(lax.ppermute(message, AXES[axis], route))  8.77 us
    pallas_call x15, Pallas kernels, call(): pl.pallas_call(body, out_shape=shapes, in_specs=in_specs, out_specs=[pl.B...  7.62 us
  transfers between devices with their start and end apart: 25, of which 5 were waited for; matrix products, arithmetic and copies ran while one was open for 0% of the time, Pallas kernels for 3%

commit v1 on v0

--- a/solution.py
+++ b/solution.py
@@ -80,15 +80,7 @@
         write_messages(lengths, vecs, blocks, sends, (axis,))
 
 
-def interior(lengths, first_core, vecs, onsite, blocks, *totals):
-    total = totals[-1]
-
-    @pl.when(is_even_on(2) == first_core)
-    def _():
-        interior_sums(lengths, vecs, onsite, blocks, total)
-
-
-def interior_sums(lengths, vecs, onsite, blocks, total):
+def interior(lengths, vecs, onsite, blocks, total):
     for p in places(lengths):
         c = number(p, lengths)
         vs, ms, ws, ns = [vecs[c]], [onsite[c]], [], []
@@ -144,7 +136,7 @@
         copy.wait()
 
 
-def call(body, operands, shapes, flops, place=pltpu.VMEM, scratch=(), aliases={}):
+def call(body, operands, shapes, flops, place=pltpu.VMEM, scratch=()):
     in_specs = [pl.BlockSpec(memory_space=pltpu.VMEM)] * len(operands)
     moved = sum(a.size * a.dtype.itemsize for a in operands) + sum(s.size * s.dtype.itemsize for s in shapes)
     return pl.pallas_call(
@@ -153,7 +145,6 @@
         in_specs=in_specs,
         out_specs=[pl.BlockSpec(memory_space=place)] * len(shapes),
         scratch_shapes=scratch,
-        input_output_aliases=aliases,
         cost_estimate=pl.CostEstimate(flops=flops, bytes_accessed=moved, transcendentals=0),
         compiler_params=pltpu.CompilerParams(vmem_limit_bytes=24 << 20),
     )(*operands)
@@ -208,10 +199,11 @@
     for step in range(STEPS):
         last = step == STEPS - 1
         got = exchanged(sends)
-        sums, inside = [jax.ShapeDtypeStruct((cells, k, q), F32)], (7 * cells - 2 * faces) * one
-        total = call(lambda *r: interior(lengths, False, *r), [vecs, onsite, blocks], sums, inside)
         (total,) = call(
-            lambda *r: interior(lengths, True, *r), [vecs, onsite, blocks, *total], sums, inside, aliases={3: 0}
+            lambda *r: interior(lengths, *r),
+            [vecs, onsite, blocks],
+            [jax.ShapeDtypeStruct((cells, k, q), F32)],
+            (7 * cells - 2 * faces) * one,
         )
         result = jax.ShapeDtypeStruct((cells, k, q), F32 if last else BF16)
         following, *sends = call(

time: 113 us -> 113 us (level)
    pallas_call x15 -> x10, Pallas kernels: 7.62 us -> 7.49 us  [call(): pl.pallas_call(body, out_shape=shapes, in_specs=in_specs, out_specs=[pl.B...]
where the time goes in v1:
time: 113 us; the launch traced here: 112 us
  starting transfers between devices  84.1 us (74%)
  Pallas kernels  9.64 us (9%)
  blocking collectives  9.5 us (8%)
  waiting for transfers between devices  8.91 us (8%)
    ppermute x25, starting transfers between devices, exchanged(): got.append(lax.ppermute(message, AXES[axis], route))  84.1 us
    all_gather x5, blocking collectives, exchanged(): got.append(lax.all_gather(message, AXES[axis], axis_index_groups=pairs))  9.5 us
    ppermute x25, waiting for transfers between devices, exchanged(): got.append(lax.ppermute(message, AXES[axis], route))  8.91 us
    pallas_call x10, Pallas kernels, call(): pl.pallas_call(body, out_shape=shapes, in_specs=in_specs, out_specs=[pl.B...  7.49 us
  transfers between devices with their start and end apart: 25, of which 5 were waited for; matrix products, arithmetic and copies ran while one was open for 0% of the time, Pallas kernels for 3%

profile of v1, /device:TPU:407, one launch (start us, length us, event | category | flops | bytes accessed | tf_op | source)
XLA Modules:
  0.0 112.4 jit_solution(13368749919669520570)
XLA Ops:
  0.0 2.2 %prepare.1 = (bf16[16,64,128]{2,1,0:T(8,128)(2,1)S(1)}, bf16[3,16,128,128]{3,2,1,0:T(8,128)(2,1)S(1)}, bf16[8,64,128]{2,1,0:T(8,128)(2,1)S(1)}, bf16[8,64,128]{2...) custom-call(s32[3,2,2,4]{3,2,1,0:T(2,128)} %r_0_.1, ...), custom_call_target="tpu_custom_call" | custom-call | flops 41943040 | bytes 4194304 | tf_op jit(solution)/shard_map/prepare/pallas_call | solution.py:188
  2.2 2.0 %collective-permute-start = (bf16[8,64,128]{2,1,0:T(8,128)(2,1)S(1)}, bf16[8,64,128]{2,1,0:T(8,128)(2,1)S(1)}, u32[]{:S(2)}, u32[]{:S(2)}) collective-permute-start(bf16[8,64,128]{2,1,0:T(8,128)(2,1)S(1)} %get-tuple-element.43), channel_id=1, source_target_pairs={{0,128},{256,384},{512,640},{768,896},{128,0},{384,256},{640,512},... | collective-permute-start | bytes 393224 | tf_op jit(solution)/shard_map/ppermute | solution.py:170
  4.1 4.7 %collective-permute-start.1 = (bf16[8,64,128]{2,1,0:T(8,128)(2,1)S(1)}, bf16[8,64,128]{2,1,0:T(8,128)(2,1)S(1)}, u32[]{:S(2)}, u32[]{:S(2)}) collective-permute-start(bf16[8,64,128]{2,1,0:T(8,128)(2,1)S(1)} %get-tuple-element.44), channel_id=1, source_target_pairs={{128,256},{384,512},{640,768},{256,128},{512,384},{768,640},{129,2... | collective-permute-start | bytes 393224 | tf_op jit(solution)/shard_map/ppermute | solution.py:170
  8.8 2.1 %collective-permute-start.2 = (bf16[8,64,128]{2,1,0:T(8,128)(2,1)S(1)}, bf16[8,64,128]{2,1,0:T(8,128)(2,1)S(1)}, u32[]{:S(2)}, u32[]{:S(2)}) collective-permute-start(bf16[8,64,128]{2,1,0:T(8,128)(2,1)S(1)} %get-tuple-element.45), channel_id=1, source_target_pairs={{0,32},{64,96},{32,0},{96,64},{1,33},{65,97},{33,1},{97,65},{2,34}... | collective-permute-start | bytes 393224 | tf_op jit(solution)/shard_map/ppermute | solution.py:170
  11.0 4.5 %collective-permute-start.3 = (bf16[8,64,128]{2,1,0:T(8,128)(2,1)S(1)}, bf16[8,64,128]{2,1,0:T(8,128)(2,1)S(1)}, u32[]{:S(2)}, u32[]{:S(2)}) collective-permute-start(bf16[8,64,128]{2,1,0:T(8,128)(2,1)S(1)} %get-tuple-element.46), channel_id=1, source_target_pairs={{32,64},{64,32},{33,65},{65,33},{34,66},{66,34},{35,67},{67,35},{3... | collective-permute-start | bytes 393224 | tf_op jit(solution)/shard_map/ppermute | solution.py:170
  15.4 8.7 %collective-permute-start.4 = (bf16[4,64,128]{2,1,0:T(8,128)(2,1)S(1)}, bf16[4,64,128]{2,1,0:T(8,128)(2,1)S(1)}, u32[]{:S(2)}, u32[]{:S(2)}) collective-permute-start(bf16[4,64,128]{2,1,0:T(8,128)(2,1)S(1)} %get-tuple-element.48), channel_id=1, source_target_pairs={{1,2},{3,4},{5,6},{7,8},{9,10},{11,12},{13,14},{15,16},{17,18},{19... | collective-permute-start | bytes 196616 | tf_op jit(solution)/shard_map/ppermute | solution.py:170
  24.1 0.7 shard_map.46.r_0_
  24.9 1.9 %all-gather = bf16[8,64,128]{2,1,0:T(8,128)(2,1)S(1)} all-gather(bf16[4,64,128]{2,1,0:T(8,128)(2,1)S(1)} %get-tuple-element.47), channel_id=2, replica_groups={{0,1},{2,3},{4,5},{6,7},{8,9},{10,11},{12,13},{14,15},{16,17},{18,19},{..., dimensions={0}, use_global_device_ids=true | all-gather | bytes 196608 | tf_op jit(solution)/shard_map/all_gather | solution.py:168
  26.8 1.0 collective-permute-done.4.r_9_
  27.8 0.0 collective-permute-done.r_4_
  27.8 0.0 collective-permute-done.1.r_5_
  27.8 0.0 collective-permute-done.2.r_6_
  27.8 0.0 collective-permute-done.3.r_7_
  27.8 0.7 shard_map.47
  28.5 1.9 %collective-permute-start.5 = (bf16[8,64,128]{2,1,0:T(8,128)(2,1)S(1)}, bf16[8,64,128]{2,1,0:T(8,128)(2,1)S(1)}, u32[]{:S(2)}, u32[]{:S(2)}) collective-permute-start(bf16[8,64,128]{2,1,0:T(8,128)(2,1)S(1)} %get-tuple-element.50), channel_id=1, source_target_pairs={{0,128},{256,384},{512,640},{768,896},{128,0},{384,256},{640,512},... | collective-permute-start | bytes 393224 | tf_op jit(solution)/shard_map/ppermute | solution.py:170
  30.4 5.0 %collective-permute-start.6 = (bf16[8,64,128]{2,1,0:T(8,128)(2,1)S(1)}, bf16[8,64,128]{2,1,0:T(8,128)(2,1)S(1)}, u32[]{:S(2)}, u32[]{:S(2)}) collective-permute-start(bf16[8,64,128]{2,1,0:T(8,128)(2,1)S(1)} %get-tuple-element.51), channel_id=1, source_target_pairs={{128,256},{384,512},{640,768},{256,128},{512,384},{768,640},{129,2... | collective-permute-start | bytes 393224 | tf_op jit(solution)/shard_map/ppermute | solution.py:170
  35.5 1.9 %collective-permute-start.7 = (bf16[8,64,128]{2,1,0:T(8,128)(2,1)S(1)}, bf16[8,64,128]{2,1,0:T(8,128)(2,1)S(1)}, u32[]{:S(2)}, u32[]{:S(2)}) collective-permute-start(bf16[8,64,128]{2,1,0:T(8,128)(2,1)S(1)} %get-tuple-element.52), channel_id=1, source_target_pairs={{0,32},{64,96},{32,0},{96,64},{1,33},{65,97},{33,1},{97,65},{2,34}... | collective-permute-start | bytes 393224 | tf_op jit(solution)/shard_map/ppermute | solution.py:170
  37.4 1.9 %collective-permute-start.8 = (bf16[8,64,128]{2,1,0:T(8,128)(2,1)S(1)}, bf16[8,64,128]{2,1,0:T(8,128)(2,1)S(1)}, u32[]{:S(2)}, u32[]{:S(2)}) collective-permute-start(bf16[8,64,128]{2,1,0:T(8,128)(2,1)S(1)} %get-tuple-element.53), channel_id=1, source_target_pairs={{32,64},{64,32},{33,65},{65,33},{34,66},{66,34},{35,67},{67,35},{3... | collective-permute-start | bytes 393224 | tf_op jit(solution)/shard_map/ppermute | solution.py:170
  39.3 5.6 %collective-permute-start.9 = (bf16[4,64,128]{2,1,0:T(8,128)(2,1)S(1)}, bf16[4,64,128]{2,1,0:T(8,128)(2,1)S(1)}, u32[]{:S(2)}, u32[]{:S(2)}) collective-permute-start(bf16[4,64,128]{2,1,0:T(8,128)(2,1)S(1)} %get-tuple-element.55), channel_id=1, source_target_pairs={{1,2},{3,4},{5,6},{7,8},{9,10},{11,12},{13,14},{15,16},{17,18},{19... | collective-permute-start | bytes 196616 | tf_op jit(solution)/shard_map/ppermute | solution.py:170
  44.9 0.7 shard_map.48.r_0_
  45.7 1.9 %all-gather.1 = bf16[8,64,128]{2,1,0:T(8,128)(2,1)S(1)} all-gather(bf16[4,64,128]{2,1,0:T(8,128)(2,1)S(1)} %get-tuple-element.54), channel_id=3, replica_groups={{0,1},{2,3},{4,5},{6,7},{8,9},{10,11},{12,13},{14,15},{16,17},{18,19},{..., dimensions={0}, use_global_device_ids=true | all-gather | bytes 196608 | tf_op jit(solution)/shard_map/all_gather | solution.py:168
  47.6 2.0 %collective-permute-done.9.r_9_ = bf16[4,64,128]{2,1,0:T(8,128)(2,1)S(1)} collective-permute-done((bf16[4,64,128]{2,1,0:T(8,128)(2,1)S(1)}, bf16[4,64,128]{2,1,0:T(8,128)(2,1)S(1)}, u32[]{:S(2)}, u32[]{:S(2)}) %collective-permute-start.9) | collective-permute-done | bytes 65568 | tf_op jit(solution)/shard_map/ppermute | solution.py:170
  49.6 0.0 collective-permute-done.5.r_4_
  49.6 0.0 collective-permute-done.6.r_5_
  49.6 0.0 collective-permute-done.7.r_6_
  49.6 0.0 collective-permute-done.8.r_7_
  49.6 0.7 shard_map.49
  50.3 1.9 %collective-permute-start.10 = (bf16[8,64,128]{2,1,0:T(8,128)(2,1)S(1)}, bf16[8,64,128]{2,1,0:T(8,128)(2,1)S(1)}, u32[]{:S(2)}, u32[]{:S(2)}) collective-permute-start(bf16[8,64,128]{2,1,0:T(8,128)(2,1)S(1)} %get-tuple-element.57), channel_id=1, source_target_pairs={{0,128},{256,384},{512,640},{768,896},{128,0},{384,256},{640,512},... | collective-permute-start | bytes 393224 | tf_op jit(solution)/shard_map/ppermute | solution.py:170
  52.2 2.9 %collective-permute-start.11 = (bf16[8,64,128]{2,1,0:T(8,128)(2,1)S(1)}, bf16[8,64,128]{2,1,0:T(8,128)(2,1)S(1)}, u32[]{:S(2)}, u32[]{:S(2)}) collective-permute-start(bf16[8,64,128]{2,1,0:T(8,128)(2,1)S(1)} %get-tuple-element.58), channel_id=1, source_target_pairs={{128,256},{384,512},{640,768},{256,128},{512,384},{768,640},{129,2... | collective-permute-start | bytes 393224 | tf_op jit(solution)/shard_map/ppermute | solution.py:170
  55.1 1.9 %collective-permute-start.12 = (bf16[8,64,128]{2,1,0:T(8,128)(2,1)S(1)}, bf16[8,64,128]{2,1,0:T(8,128)(2,1)S(1)}, u32[]{:S(2)}, u32[]{:S(2)}) collective-permute-start(bf16[8,64,128]{2,1,0:T(8,128)(2,1)S(1)} %get-tuple-element.59), channel_id=1, source_target_pairs={{0,32},{64,96},{32,0},{96,64},{1,33},{65,97},{33,1},{97,65},{2,34}... | collective-permute-start | bytes 393224 | tf_op jit(solution)/shard_map/ppermute | solution.py:170
  57.1 3.8 %collective-permute-start.13 = (bf16[8,64,128]{2,1,0:T(8,128)(2,1)S(1)}, bf16[8,64,128]{2,1,0:T(8,128)(2,1)S(1)}, u32[]{:S(2)}, u32[]{:S(2)}) collective-permute-start(bf16[8,64,128]{2,1,0:T(8,128)(2,1)S(1)} %get-tuple-element.60), channel_id=1, source_target_pairs={{32,64},{64,32},{33,65},{65,33},{34,66},{66,34},{35,67},{67,35},{3... | collective-permute-start | bytes 393224 | tf_op jit(solution)/shard_map/ppermute | solution.py:170
  60.8 4.9 %collective-permute-start.14 = (bf16[4,64,128]{2,1,0:T(8,128)(2,1)S(1)}, bf16[4,64,128]{2,1,0:T(8,128)(2,1)S(1)}, u32[]{:S(2)}, u32[]{:S(2)}) collective-permute-start(bf16[4,64,128]{2,1,0:T(8,128)(2,1)S(1)} %get-tuple-element.62), channel_id=1, source_target_pairs={{1,2},{3,4},{5,6},{7,8},{9,10},{11,12},{13,14},{15,16},{17,18},{19... | collective-permute-start | bytes 196616 | tf_op jit(solution)/shard_map/ppermute | solution.py:170
  65.7 0.7 shard_map.50.r_0_
  66.4 1.9 %all-gather.2 = bf16[8,64,128]{2,1,0:T(8,128)(2,1)S(1)} all-gather(bf16[4,64,128]{2,1,0:T(8,128)(2,1)S(1)} %get-tuple-element.61), channel_id=4, replica_groups={{0,1},{2,3},{4,5},{6,7},{8,9},{10,11},{12,13},{14,15},{16,17},{18,19},{..., dimensions={0}, use_global_device_ids=true | all-gather | bytes 196608 | tf_op jit(solution)/shard_map/all_gather | solution.py:168
  68.3 2.1 %collective-permute-done.14.r_9_ = bf16[4,64,128]{2,1,0:T(8,128)(2,1)S(1)} collective-permute-done((bf16[4,64,128]{2,1,0:T(8,128)(2,1)S(1)}, bf16[4,64,128]{2,1,0:T(8,128)(2,1)S(1)}, u32[]{:S(2)}, u32[]{:S(2)}) %collective-permute-start.14) | collective-permute-done | bytes 65568 | tf_op jit(solution)/shard_map/ppermute | solution.py:170
  70.5 0.0 collective-permute-done.10.r_4_
  70.5 0.0 collective-permute-done.11.r_5_
  70.5 0.0 collective-permute-done.12.r_6_
  70.5 0.0 collective-permute-done.13.r_7_
  70.5 0.7 shard_map.51
  71.2 1.9 %collective-permute-start.15 = (bf16[8,64,128]{2,1,0:T(8,128)(2,1)S(1)}, bf16[8,64,128]{2,1,0:T(8,128)(2,1)S(1)}, u32[]{:S(2)}, u32[]{:S(2)}) collective-permute-start(bf16[8,64,128]{2,1,0:T(8,128)(2,1)S(1)} %get-tuple-element.64), channel_id=1, source_target_pairs={{0,128},{256,384},{512,640},{768,896},{128,0},{384,256},{640,512},... | collective-permute-start | bytes 393224 | tf_op jit(solution)/shard_map/ppermute | solution.py:170
  73.1 3.4 %collective-permute-start.16 = (bf16[8,64,128]{2,1,0:T(8,128)(2,1)S(1)}, bf16[8,64,128]{2,1,0:T(8,128)(2,1)S(1)}, u32[]{:S(2)}, u32[]{:S(2)}) collective-permute-start(bf16[8,64,128]{2,1,0:T(8,128)(2,1)S(1)} %get-tuple-element.65), channel_id=1, source_target_pairs={{128,256},{384,512},{640,768},{256,128},{512,384},{768,640},{129,2... | collective-permute-start | bytes 393224 | tf_op jit(solution)/shard_map/ppermute | solution.py:170
  76.5 1.9 %collective-permute-start.17 = (bf16[8,64,128]{2,1,0:T(8,128)(2,1)S(1)}, bf16[8,64,128]{2,1,0:T(8,128)(2,1)S(1)}, u32[]{:S(2)}, u32[]{:S(2)}) collective-permute-start(bf16[8,64,128]{2,1,0:T(8,128)(2,1)S(1)} %get-tuple-element.66), channel_id=1, source_target_pairs={{0,32},{64,96},{32,0},{96,64},{1,33},{65,97},{33,1},{97,65},{2,34}... | collective-permute-start | bytes 393224 | tf_op jit(solution)/shard_map/ppermute | solution.py:170
  78.4 2.6 %collective-permute-start.18 = (bf16[8,64,128]{2,1,0:T(8,128)(2,1)S(1)}, bf16[8,64,128]{2,1,0:T(8,128)(2,1)S(1)}, u32[]{:S(2)}, u32[]{:S(2)}) collective-permute-start(bf16[8,64,128]{2,1,0:T(8,128)(2,1)S(1)} %get-tuple-element.67), channel_id=1, source_target_pairs={{32,64},{64,32},{33,65},{65,33},{34,66},{66,34},{35,67},{67,35},{3... | collective-permute-start | bytes 393224 | tf_op jit(solution)/shard_map/ppermute | solution.py:170
  81.0 4.9 %collective-permute-start.19 = (bf16[4,64,128]{2,1,0:T(8,128)(2,1)S(1)}, bf16[4,64,128]{2,1,0:T(8,128)(2,1)S(1)}, u32[]{:S(2)}, u32[]{:S(2)}) collective-permute-start(bf16[4,64,128]{2,1,0:T(8,128)(2,1)S(1)} %get-tuple-element.69), channel_id=1, source_target_pairs={{1,2},{3,4},{5,6},{7,8},{9,10},{11,12},{13,14},{15,16},{17,18},{19... | collective-permute-start | bytes 196616 | tf_op jit(solution)/shard_map/ppermute | solution.py:170
  85.9 0.7 shard_map.52.r_0_
  86.6 1.9 %all-gather.3 = bf16[8,64,128]{2,1,0:T(8,128)(2,1)S(1)} all-gather(bf16[4,64,128]{2,1,0:T(8,128)(2,1)S(1)} %get-tuple-element.68), channel_id=5, replica_groups={{0,1},{2,3},{4,5},{6,7},{8,9},{10,11},{12,13},{14,15},{16,17},{18,19},{..., dimensions={0}, use_global_device_ids=true | all-gather | bytes 196608 | tf_op jit(solution)/shard_map/all_gather | solution.py:168
  88.5 1.8 %collective-permute-done.19.r_9_ = bf16[4,64,128]{2,1,0:T(8,128)(2,1)S(1)} collective-permute-done((bf16[4,64,128]{2,1,0:T(8,128)(2,1)S(1)}, bf16[4,64,128]{2,1,0:T(8,128)(2,1)S(1)}, u32[]{:S(2)}, u32[]{:S(2)}) %collective-permute-start.19) | collective-permute-done | bytes 65568 | tf_op jit(solution)/shard_map/ppermute | solution.py:170
  90.3 0.0 collective-permute-done.16.r_5_
  90.3 0.0 collective-permute-done.17.r_6_
  90.3 0.0 collective-permute-done.18.r_7_
  90.3 0.7 shard_map.53
  91.0 1.9 %collective-permute-start.20 = (bf16[8,64,128]{2,1,0:T(8,128)(2,1)S(1)}, bf16[8,64,128]{2,1,0:T(8,128)(2,1)S(1)}, u32[]{:S(2)}, u32[]{:S(2)}) collective-permute-start(bf16[8,64,128]{2,1,0:T(8,128)(2,1)S(1)} %get-tuple-element.71), channel_id=1, source_target_pairs={{0,128},{256,384},{512,640},{768,896},{128,0},{384,256},{640,512},... | collective-permute-start | bytes 393224 | tf_op jit(solution)/shard_map/ppermute | solution.py:170
  93.0 3.8 %collective-permute-start.21 = (bf16[8,64,128]{2,1,0:T(8,128)(2,1)S(1)}, bf16[8,64,128]{2,1,0:T(8,128)(2,1)S(1)}, u32[]{:S(2)}, u32[]{:S(2)}) collective-permute-start(bf16[8,64,128]{2,1,0:T(8,128)(2,1)S(1)} %get-tuple-element.72), channel_id=1, source_target_pairs={{128,256},{384,512},{640,768},{256,128},{512,384},{768,640},{129,2... | collective-permute-start | bytes 393224 | tf_op jit(solution)/shard_map/ppermute | solution.py:170
  96.7 1.9 %collective-permute-start.22 = (bf16[8,64,128]{2,1,0:T(8,128)(2,1)S(1)}, bf16[8,64,128]{2,1,0:T(8,128)(2,1)S(1)}, u32[]{:S(2)}, u32[]{:S(2)}) collective-permute-start(bf16[8,64,128]{2,1,0:T(8,128)(2,1)S(1)} %get-tuple-element.73), channel_id=1, source_target_pairs={{0,32},{64,96},{32,0},{96,64},{1,33},{65,97},{33,1},{97,65},{2,34}... | collective-permute-start | bytes 393224 | tf_op jit(solution)/shard_map/ppermute | solution.py:170
  98.7 2.8 %collective-permute-start.23 = (bf16[8,64,128]{2,1,0:T(8,128)(2,1)S(1)}, bf16[8,64,128]{2,1,0:T(8,128)(2,1)S(1)}, u32[]{:S(2)}, u32[]{:S(2)}) collective-permute-start(bf16[8,64,128]{2,1,0:T(8,128)(2,1)S(1)} %get-tuple-element.74), channel_id=1, source_target_pairs={{32,64},{64,32},{33,65},{65,33},{34,66},{66,34},{35,67},{67,35},{3... | collective-permute-start | bytes 393224 | tf_op jit(solution)/shard_map/ppermute | solution.py:170
  101.5 5.3 %collective-permute-start.24 = (bf16[4,64,128]{2,1,0:T(8,128)(2,1)S(1)}, bf16[4,64,128]{2,1,0:T(8,128)(2,1)S(1)}, u32[]{:S(2)}, u32[]{:S(2)}) collective-permute-start(bf16[4,64,128]{2,1,0:T(8,128)(2,1)S(1)} %get-tuple-element.76), channel_id=1, source_target_pairs={{1,2},{3,4},{5,6},{7,8},{9,10},{11,12},{13,14},{15,16},{17,18},{19... | collective-permute-start | bytes 196616 | tf_op jit(solution)/shard_map/ppermute | solution.py:170
  106.7 0.7 shard_map.54.r_0_
  107.5 1.9 %all-gather.4 = bf16[8,64,128]{2,1,0:T(8,128)(2,1)S(1)} all-gather(bf16[4,64,128]{2,1,0:T(8,128)(2,1)S(1)} %get-tuple-element.75), channel_id=6, replica_groups={{0,1},{2,3},{4,5},{6,7},{8,9},{10,11},{12,13},{14,15},{16,17},{18,19},{..., dimensions={0}, use_global_device_ids=true | all-gather | bytes 196608 | tf_op jit(solution)/shard_map/all_gather | solution.py:168
  109.4 1.9 %collective-permute-done.24.r_9_ = bf16[4,64,128]{2,1,0:T(8,128)(2,1)S(1)} collective-permute-done((bf16[4,64,128]{2,1,0:T(8,128)(2,1)S(1)}, bf16[4,64,128]{2,1,0:T(8,128)(2,1)S(1)}, u32[]{:S(2)}, u32[]{:S(2)}) %collective-permute-start.24) | collective-permute-done | bytes 65568 | tf_op jit(solution)/shard_map/ppermute | solution.py:170
  111.3 0.0 collective-permute-done.21.r_5_
  111.3 0.0 collective-permute-done.22.r_6_
  111.3 0.0 collective-permute-done.23.r_7_
  111.3 1.1 %shard_map.55 = f32[16,64,128]{2,1,0:T(8,128)} custom-call(f32[16,64,128]{2,1,0:T(8,128)S(1)} %shard_map.54.r_0_, bf16[16,64,128]{2,1,0:T(8,128)(2,1)S(1)} %get-tuple-element.70.r_0_.r_1_, bf16[16,64,128]{2,1,0:T(8,128)(2,1)S(1)} %get-tuple-element.63.r_0_.r_1_.r_2_, bf16[3,16,128,128]{3,2,1,0:T(8,128)(2,1)S(1)} %get-tuple-element.42.r_2_.r_3_, ...), custom_call_target="tpu_custom_call" | custom-call | flops 41943040 | bytes 3866624 | tf_op jit(solution)/shard_map/pallas_call | solution.py:142
  (4 shorter events, 0.0 us)
Async XLA Ops:
  0.0 24.1 %copy-start = (bf16[2,2,4,128,128]{4,3,2,1,0:T(8,128)(2,1)S(1)}, bf16[2,2,4,128,128]{4,3,2,1,0:T(8,128)(2,1)}, u32[]{:S(2)}) copy-start(bf16[2,2,4,128,128]{4,3,2,1,0:T(8,128)(2,1)} %param.5) | copy-start | bytes 1572868
  2.2 25.6 %collective-permute-start = (bf16[8,64,128]{2,1,0:T(8,128)(2,1)S(1)}, bf16[8,64,128]{2,1,0:T(8,128)(2,1)S(1)}, u32[]{:S(2)}, u32[]{:S(2)}) collective-permute-start(bf16[8,64,128]{2,1,0:T(8,128)(2,1)S(1)} %get-tuple-element.43), channel_id=1, source_target_pairs={{0,128},{256,384},{512,640},{768,896},{128,0},{384,256},{640,512},... | collective-permute-start | bytes 393224 | tf_op jit(solution)/shard_map/ppermute | solution.py:170
  4.1 23.7 %collective-permute-start.1 = (bf16[8,64,128]{2,1,0:T(8,128)(2,1)S(1)}, bf16[8,64,128]{2,1,0:T(8,128)(2,1)S(1)}, u32[]{:S(2)}, u32[]{:S(2)}) collective-permute-start(bf16[8,64,128]{2,1,0:T(8,128)(2,1)S(1)} %get-tuple-element.44), channel_id=1, source_target_pairs={{128,256},{384,512},{640,768},{256,128},{512,384},{768,640},{129,2... | collective-permute-start | bytes 393224 | tf_op jit(solution)/shard_map/ppermute | solution.py:170
  8.8 19.0 %collective-permute-start.2 = (bf16[8,64,128]{2,1,0:T(8,128)(2,1)S(1)}, bf16[8,64,128]{2,1,0:T(8,128)(2,1)S(1)}, u32[]{:S(2)}, u32[]{:S(2)}) collective-permute-start(bf16[8,64,128]{2,1,0:T(8,128)(2,1)S(1)} %get-tuple-element.45), channel_id=1, source_target_pairs={{0,32},{64,96},{32,0},{96,64},{1,33},{65,97},{33,1},{97,65},{2,34}... | collective-permute-start | bytes 393224 | tf_op jit(solution)/shard_map/ppermute | solution.py:170
  11.0 16.9 %collective-permute-start.3 = (bf16[8,64,128]{2,1,0:T(8,128)(2,1)S(1)}, bf16[8,64,128]{2,1,0:T(8,128)(2,1)S(1)}, u32[]{:S(2)}, u32[]{:S(2)}) collective-permute-start(bf16[8,64,128]{2,1,0:T(8,128)(2,1)S(1)} %get-tuple-element.46), channel_id=1, source_target_pairs={{32,64},{64,32},{33,65},{65,33},{34,66},{66,34},{35,67},{67,35},{3... | collective-permute-start | bytes 393224 | tf_op jit(solution)/shard_map/ppermute | solution.py:170
  15.4 12.4 %collective-permute-start.4 = (bf16[4,64,128]{2,1,0:T(8,128)(2,1)S(1)}, bf16[4,64,128]{2,1,0:T(8,128)(2,1)S(1)}, u32[]{:S(2)}, u32[]{:S(2)}) collective-permute-start(bf16[4,64,128]{2,1,0:T(8,128)(2,1)S(1)} %get-tuple-element.48), channel_id=1, source_target_pairs={{1,2},{3,4},{5,6},{7,8},{9,10},{11,12},{13,14},{15,16},{17,18},{19... | collective-permute-start | bytes 196616 | tf_op jit(solution)/shard_map/ppermute | solution.py:170
  28.5 21.1 %collective-permute-start.5 = (bf16[8,64,128]{2,1,0:T(8,128)(2,1)S(1)}, bf16[8,64,128]{2,1,0:T(8,128)(2,1)S(1)}, u32[]{:S(2)}, u32[]{:S(2)}) collective-permute-start(bf16[8,64,128]{2,1,0:T(8,128)(2,1)S(1)} %get-tuple-element.50), channel_id=1, source_target_pairs={{0,128},{256,384},{512,640},{768,896},{128,0},{384,256},{640,512},... | collective-permute-start | bytes 393224 | tf_op jit(solution)/shard_map/ppermute | solution.py:170
  30.4 19.1 %collective-permute-start.6 = (bf16[8,64,128]{2,1,0:T(8,128)(2,1)S(1)}, bf16[8,64,128]{2,1,0:T(8,128)(2,1)S(1)}, u32[]{:S(2)}, u32[]{:S(2)}) collective-permute-start(bf16[8,64,128]{2,1,0:T(8,128)(2,1)S(1)} %get-tuple-element.51), channel_id=1, source_target_pairs={{128,256},{384,512},{640,768},{256,128},{512,384},{768,640},{129,2... | collective-permute-start | bytes 393224 | tf_op jit(solution)/shard_map/ppermute | solution.py:170
  35.5 14.1 %collective-permute-start.7 = (bf16[8,64,128]{2,1,0:T(8,128)(2,1)S(1)}, bf16[8,64,128]{2,1,0:T(8,128)(2,1)S(1)}, u32[]{:S(2)}, u32[]{:S(2)}) collective-permute-start(bf16[8,64,128]{2,1,0:T(8,128)(2,1)S(1)} %get-tuple-element.52), channel_id=1, source_target_pairs={{0,32},{64,96},{32,0},{96,64},{1,33},{65,97},{33,1},{97,65},{2,34}... | collective-permute-start | bytes 393224 | tf_op jit(solution)/shard_map/ppermute | solution.py:170
  37.4 12.2 %collective-permute-start.8 = (bf16[8,64,128]{2,1,0:T(8,128)(2,1)S(1)}, bf16[8,64,128]{2,1,0:T(8,128)(2,1)S(1)}, u32[]{:S(2)}, u32[]{:S(2)}) collective-permute-start(bf16[8,64,128]{2,1,0:T(8,128)(2,1)S(1)} %get-tuple-element.53), channel_id=1, source_target_pairs={{32,64},{64,32},{33,65},{65,33},{34,66},{66,34},{35,67},{67,35},{3... | collective-permute-start | bytes 393224 | tf_op jit(solution)/shard_map/ppermute | solution.py:170
  39.3 10.2 %collective-permute-start.9 = (bf16[4,64,128]{2,1,0:T(8,128)(2,1)S(1)}, bf16[4,64,128]{2,1,0:T(8,128)(2,1)S(1)}, u32[]{:S(2)}, u32[]{:S(2)}) collective-permute-start(bf16[4,64,128]{2,1,0:T(8,128)(2,1)S(1)} %get-tuple-element.55), channel_id=1, source_target_pairs={{1,2},{3,4},{5,6},{7,8},{9,10},{11,12},{13,14},{15,16},{17,18},{19... | collective-permute-start | bytes 196616 | tf_op jit(solution)/shard_map/ppermute | solution.py:170
  50.3 20.2 %collective-permute-start.10 = (bf16[8,64,128]{2,1,0:T(8,128)(2,1)S(1)}, bf16[8,64,128]{2,1,0:T(8,128)(2,1)S(1)}, u32[]{:S(2)}, u32[]{:S(2)}) collective-permute-start(bf16[8,64,128]{2,1,0:T(8,128)(2,1)S(1)} %get-tuple-element.57), channel_id=1, source_target_pairs={{0,128},{256,384},{512,640},{768,896},{128,0},{384,256},{640,512},... | collective-permute-start | bytes 393224 | tf_op jit(solution)/shard_map/ppermute | solution.py:170
  52.2 18.2 %collective-permute-start.11 = (bf16[8,64,128]{2,1,0:T(8,128)(2,1)S(1)}, bf16[8,64,128]{2,1,0:T(8,128)(2,1)S(1)}, u32[]{:S(2)}, u32[]{:S(2)}) collective-permute-start(bf16[8,64,128]{2,1,0:T(8,128)(2,1)S(1)} %get-tuple-element.58), channel_id=1, source_target_pairs={{128,256},{384,512},{640,768},{256,128},{512,384},{768,640},{129,2... | collective-permute-start | bytes 393224 | tf_op jit(solution)/shard_map/ppermute | solution.py:170
  55.1 15.3 %collective-permute-start.12 = (bf16[8,64,128]{2,1,0:T(8,128)(2,1)S(1)}, bf16[8,64,128]{2,1,0:T(8,128)(2,1)S(1)}, u32[]{:S(2)}, u32[]{:S(2)}) collective-permute-start(bf16[8,64,128]{2,1,0:T(8,128)(2,1)S(1)} %get-tuple-element.59), channel_id=1, source_target_pairs={{0,32},{64,96},{32,0},{96,64},{1,33},{65,97},{33,1},{97,65},{2,34}... | collective-permute-start | bytes 393224 | tf_op jit(solution)/shard_map/ppermute | solution.py:170
  57.1 13.4 %collective-permute-start.13 = (bf16[8,64,128]{2,1,0:T(8,128)(2,1)S(1)}, bf16[8,64,128]{2,1,0:T(8,128)(2,1)S(1)}, u32[]{:S(2)}, u32[]{:S(2)}) collective-permute-start(bf16[8,64,128]{2,1,0:T(8,128)(2,1)S(1)} %get-tuple-element.60), channel_id=1, source_target_pairs={{32,64},{64,32},{33,65},{65,33},{34,66},{66,34},{35,67},{67,35},{3... | collective-permute-start | bytes 393224 | tf_op jit(solution)/shard_map/ppermute | solution.py:170
  60.8 9.6 %collective-permute-start.14 = (bf16[4,64,128]{2,1,0:T(8,128)(2,1)S(1)}, bf16[4,64,128]{2,1,0:T(8,128)(2,1)S(1)}, u32[]{:S(2)}, u32[]{:S(2)}) collective-permute-start(bf16[4,64,128]{2,1,0:T(8,128)(2,1)S(1)} %get-tuple-element.62), channel_id=1, source_target_pairs={{1,2},{3,4},{5,6},{7,8},{9,10},{11,12},{13,14},{15,16},{17,18},{19... | collective-permute-start | bytes 196616 | tf_op jit(solution)/shard_map/ppermute | solution.py:170
  71.2 19.2 %collective-permute-start.15 = (bf16[8,64,128]{2,1,0:T(8,128)(2,1)S(1)}, bf16[8,64,128]{2,1,0:T(8,128)(2,1)S(1)}, u32[]{:S(2)}, u32[]{:S(2)}) collective-permute-start(bf16[8,64,128]{2,1,0:T(8,128)(2,1)S(1)} %get-tuple-element.64), channel_id=1, source_target_pairs={{0,128},{256,384},{512,640},{768,896},{128,0},{384,256},{640,512},... | collective-permute-start | bytes 393224 | tf_op jit(solution)/shard_map/ppermute | solution.py:170
  73.1 17.2 %collective-permute-start.16 = (bf16[8,64,128]{2,1,0:T(8,128)(2,1)S(1)}, bf16[8,64,128]{2,1,0:T(8,128)(2,1)S(1)}, u32[]{:S(2)}, u32[]{:S(2)}) collective-permute-start(bf16[8,64,128]{2,1,0:T(8,128)(2,1)S(1)} %get-tuple-element.65), channel_id=1, source_target_pairs={{128,256},{384,512},{640,768},{256,128},{512,384},{768,640},{129,2... | collective-permute-start | bytes 393224 | tf_op jit(solution)/shard_map/ppermute | solution.py:170
  76.5 13.8 %collective-permute-start.17 = (bf16[8,64,128]{2,1,0:T(8,128)(2,1)S(1)}, bf16[8,64,128]{2,1,0:T(8,128)(2,1)S(1)}, u32[]{:S(2)}, u32[]{:S(2)}) collective-permute-start(bf16[8,64,128]{2,1,0:T(8,128)(2,1)S(1)} %get-tuple-element.66), channel_id=1, source_target_pairs={{0,32},{64,96},{32,0},{96,64},{1,33},{65,97},{33,1},{97,65},{2,34}... | collective-permute-start | bytes 393224 | tf_op jit(solution)/shard_map/ppermute | solution.py:170
  78.4 11.9 %collective-permute-start.18 = (bf16[8,64,128]{2,1,0:T(8,128)(2,1)S(1)}, bf16[8,64,128]{2,1,0:T(8,128)(2,1)S(1)}, u32[]{:S(2)}, u32[]{:S(2)}) collective-permute-start(bf16[8,64,128]{2,1,0:T(8,128)(2,1)S(1)} %get-tuple-element.67), channel_id=1, source_target_pairs={{32,64},{64,32},{33,65},{65,33},{34,66},{66,34},{35,67},{67,35},{3... | collective-permute-start | bytes 393224 | tf_op jit(solution)/shard_map/ppermute | solution.py:170
  81.0 9.3 %collective-permute-start.19 = (bf16[4,64,128]{2,1,0:T(8,128)(2,1)S(1)}, bf16[4,64,128]{2,1,0:T(8,128)(2,1)S(1)}, u32[]{:S(2)}, u32[]{:S(2)}) collective-permute-start(bf16[4,64,128]{2,1,0:T(8,128)(2,1)S(1)} %get-tuple-element.69), channel_id=1, source_target_pairs={{1,2},{3,4},{5,6},{7,8},{9,10},{11,12},{13,14},{15,16},{17,18},{19... | collective-permute-start | bytes 196616 | tf_op jit(solution)/shard_map/ppermute | solution.py:170
  91.0 20.2 %collective-permute-start.20 = (bf16[8,64,128]{2,1,0:T(8,128)(2,1)S(1)}, bf16[8,64,128]{2,1,0:T(8,128)(2,1)S(1)}, u32[]{:S(2)}, u32[]{:S(2)}) collective-permute-start(bf16[8,64,128]{2,1,0:T(8,128)(2,1)S(1)} %get-tuple-element.71), channel_id=1, source_target_pairs={{0,128},{256,384},{512,640},{768,896},{128,0},{384,256},{640,512},... | collective-permute-start | bytes 393224 | tf_op jit(solution)/shard_map/ppermute | solution.py:170
  93.0 18.3 %collective-permute-start.21 = (bf16[8,64,128]{2,1,0:T(8,128)(2,1)S(1)}, bf16[8,64,128]{2,1,0:T(8,128)(2,1)S(1)}, u32[]{:S(2)}, u32[]{:S(2)}) collective-permute-start(bf16[8,64,128]{2,1,0:T(8,128)(2,1)S(1)} %get-tuple-element.72), channel_id=1, source_target_pairs={{128,256},{384,512},{640,768},{256,128},{512,384},{768,640},{129,2... | collective-permute-start | bytes 393224 | tf_op jit(solution)/shard_map/ppermute | solution.py:170
  96.7 14.6 %collective-permute-start.22 = (bf16[8,64,128]{2,1,0:T(8,128)(2,1)S(1)}, bf16[8,64,128]{2,1,0:T(8,128)(2,1)S(1)}, u32[]{:S(2)}, u32[]{:S(2)}) collective-permute-start(bf16[8,64,128]{2,1,0:T(8,128)(2,1)S(1)} %get-tuple-element.73), channel_id=1, source_target_pairs={{0,32},{64,96},{32,0},{96,64},{1,33},{65,97},{33,1},{97,65},{2,34}... | collective-permute-start | bytes 393224 | tf_op jit(solution)/shard_map/ppermute | solution.py:170
  98.7 12.6 %collective-permute-start.23 = (bf16[8,64,128]{2,1,0:T(8,128)(2,1)S(1)}, bf16[8,64,128]{2,1,0:T(8,128)(2,1)S(1)}, u32[]{:S(2)}, u32[]{:S(2)}) collective-permute-start(bf16[8,64,128]{2,1,0:T(8,128)(2,1)S(1)} %get-tuple-element.74), channel_id=1, source_target_pairs={{32,64},{64,32},{33,65},{65,33},{34,66},{66,34},{35,67},{67,35},{3... | collective-permute-start | bytes 393224 | tf_op jit(solution)/shard_map/ppermute | solution.py:170
  101.5 9.8 %collective-permute-start.24 = (bf16[4,64,128]{2,1,0:T(8,128)(2,1)S(1)}, bf16[4,64,128]{2,1,0:T(8,128)(2,1)S(1)}, u32[]{:S(2)}, u32[]{:S(2)}) collective-permute-start(bf16[4,64,128]{2,1,0:T(8,128)(2,1)S(1)} %get-tuple-element.76), channel_id=1, source_target_pairs={{1,2},{3,4},{5,6},{7,8},{9,10},{11,12},{13,14},{15,16},{17,18},{19... | collective-permute-start | bytes 196616 | tf_op jit(solution)/shard_map/ppermute | solution.py:170
